TPU v7x, 32 devices: a whole 2x2x4 slice. The times are simulated.
32 devices in a mesh: dp: 8 (over y, x, core), tensor: 4 (over z).
Axes of the slice: x: 2, y: 2, z: 4, core: 2. Of those that a mesh axis runs over, the one named last changes fastest.
Arguments:
- inputs: bfloat16 [16384, 768], P(('dp', 'tensor')), may hold values from -6 to 6
- pass_ids: int32 [16384], P(('dp', 'tensor')), may hold values from 0 to 4
- token_pos: int32 [8, 2048], P('dp'), may hold values from 0 to 1023, never falling along the last dimension, each value on 1 to 5 neighbouring positions
- pass_table: float32 [5, 768], replicated, may hold values from -3 to 3
- ln1_gain: float32 [768], replicated, may hold values from 0.5 to 1.5
- ln1_bias: float32 [768], replicated, may hold values from -2 to 2
- w_qkv: bfloat16 [768, 3, 768], P(None, None, 'tensor'), may hold values from -0.21875 to 0.21875
- q_bias: float32 [768], P('tensor'), may hold values from -3 to 3
- v_bias: float32 [768], P('tensor'), may hold values from -0.2 to 0.2
- w_out: bfloat16 [768, 768], P('tensor'), may hold values from -3 to 3
- out_bias: float32 [768], replicated, may hold values from -2 to 2
- ln2_gain: float32 [768], replicated, may hold values from 0.5 to 1.5
- ln2_bias: float32 [768], replicated, may hold values from -2 to 2
- w_up: bfloat16 [768, 3072], P(None, 'tensor'), may hold values from -0.21875 to 0.21875
- up_bias: float32 [3072], P('tensor'), may hold values from -3 to 3
- w_down: bfloat16 [3072, 768], P('tensor'), may hold values from -0.109375 to 0.109375
- down_bias: float32 [768], replicated, may hold values from -2 to 2
- cotangent: bfloat16 [16384, 768], P(('dp', 'tensor')), may hold values from -6 to 6
Outputs:
- output: bfloat16 [16384, 768], P(('dp', 'tensor'))
- input_grad: float32 [16384, 768], P(('dp', 'tensor'))
- pass_table_grad: float32 [5, 768], replicated
- ln1_gain_grad: float32 [768], replicated
- ln1_bias_grad: float32 [768], replicated
- w_qkv_grad: float32 [768, 3, 768], P(None, None, 'tensor')
- q_bias_grad: float32 [768], P('tensor')
- v_bias_grad: float32 [768], P('tensor')
- w_out_grad: float32 [768, 768], P('tensor')
- out_bias_grad: float32 [768], replicated
- ln2_gain_grad: float32 [768], replicated
- ln2_bias_grad: float32 [768], replicated
- w_up_grad: float32 [768, 3072], P(None, 'tensor')
- up_bias_grad: float32 [3072], P('tensor')
- w_down_grad: float32 [3072, 768], P('tensor')
- down_bias_grad: float32 [768], replicated
Inputs may be any that keep to these rules, and one draw needn't show every extreme that they name: Along each sequence token_pos never falls, and each value stands at 1 to 5 consecutive rows.
All inputs are finite; a program needn't handle non-finite values.
Results may differ from a plain program's by a relative error of at most 0.012.
Values may be sent and summed in bfloat16 or wider, within the bound.
A program may use at most 128 MiB of HBM per device.

v0:
```python
import jax
import jax.numpy as jnp
from jax import lax
from jax.sharding import PartitionSpec as P

D = 768
HEADS = 12
PASSES = 5


highest = lax.Precision.HIGHEST
epsilon = 1e-05


def layer_norm(values, gains, offsets):
    centered = values - jnp.mean(values, axis=-1, keepdims=True)
    variance = jnp.mean(centered * centered, axis=-1, keepdims=True)
    return centered * lax.rsqrt(variance + epsilon) * gains + offsets


def gelu_tanh(values):
    return jax.nn.gelu(values, approximate=True)


def contract_rows(left_mat, right_mat):
    return lax.dot_general(
        left_mat, right_mat, (((0,), (0,)), ((), ())), preferred_element_type=jnp.float32
    )


def contract_cols(left_mat, right_mat):
    return lax.dot_general(
        left_mat, right_mat, (((1,), (1,)), ((), ())), preferred_element_type=jnp.float32
    )


def forward_attention(query_seq, key_seq, value_seq, positions, block_rows):
    seq_count, length = positions.shape
    block_count = length // block_rows

    def forward_one_block(flat_index):
        seq_index = flat_index // block_count
        first_row = flat_index % block_count * block_rows
        key_rows = lax.dynamic_index_in_dim(key_seq, seq_index, 0, keepdims=False)
        value_rows = lax.dynamic_index_in_dim(value_seq, seq_index, 0, keepdims=False)
        pos_row = lax.dynamic_index_in_dim(positions, seq_index, 0, keepdims=False)
        query_all = lax.dynamic_index_in_dim(query_seq, seq_index, 0, keepdims=False)
        query_rows = lax.dynamic_slice_in_dim(query_all, first_row, block_rows, 0)
        query_pos = lax.dynamic_slice_in_dim(pos_row, first_row, block_rows, 0)
        scores = jnp.einsum(
            "qhd,khd->hqk", query_rows, key_rows, preferred_element_type=jnp.float32
        )
        visible = (pos_row[None, :] <= query_pos[:, None])[None]
        scores = jnp.where(visible, scores, -1e30)
        row_peak = jnp.max(scores, axis=-1, keepdims=True)
        exp_scores = jnp.exp(scores - row_peak)
        row_total = jnp.sum(exp_scores, axis=-1, keepdims=True)
        attn_probs = (exp_scores / row_total).astype(jnp.bfloat16)
        context = jnp.einsum(
            "hqk,khd->qhd", attn_probs, value_rows, preferred_element_type=jnp.float32
        )
        return (context, row_peak + jnp.log(row_total))

    return lax.map(forward_one_block, jnp.arange(seq_count * block_count))


def backward_attention(query_seq, key_seq, value_seq, grad_seq, log_totals, positions, block_rows):
    seq_count, length = positions.shape
    block_count = length // block_rows
    heads_local = query_seq.shape[2]
    lse_seq = log_totals.reshape(seq_count, block_count, heads_local, block_rows, 1)

    def one_sequence(seq_index):
        key_rows = lax.dynamic_index_in_dim(key_seq, seq_index, 0, keepdims=False)
        value_rows = lax.dynamic_index_in_dim(value_seq, seq_index, 0, keepdims=False)
        pos_row = lax.dynamic_index_in_dim(positions, seq_index, 0, keepdims=False)
        query_all = lax.dynamic_index_in_dim(query_seq, seq_index, 0, keepdims=False)
        grad_all = lax.dynamic_index_in_dim(grad_seq, seq_index, 0, keepdims=False)
        lse_all = lax.dynamic_index_in_dim(lse_seq, seq_index, 0, keepdims=False)

        def one_one_block(running, block_index):
            grad_keys, grad_values = running
            first_row = block_index * block_rows
            query_rows = lax.dynamic_slice_in_dim(query_all, first_row, block_rows, 0)
            grad_rows = lax.dynamic_slice_in_dim(grad_all, first_row, block_rows, 0)
            query_pos = lax.dynamic_slice_in_dim(pos_row, first_row, block_rows, 0)
            lse_rows = lax.dynamic_index_in_dim(lse_all, block_index, 0, keepdims=False)
            scores = jnp.einsum(
                "qhd,khd->hqk", query_rows, key_rows, preferred_element_type=jnp.float32
            )
            visible = (pos_row[None, :] <= query_pos[:, None])[None]
            attn_probs = jnp.where(visible, jnp.exp(scores - lse_rows), 0.0)
            grad_probs = jnp.einsum(
                "qhd,khd->hqk", grad_rows, value_rows, preferred_element_type=jnp.float32
            )
            row_delta = jnp.sum(attn_probs * grad_probs, axis=-1, keepdims=True)
            grad_scores = (attn_probs * (grad_probs - row_delta)).astype(jnp.bfloat16)
            grad_query = jnp.einsum(
                "hqk,khd->qhd", grad_scores, key_rows, preferred_element_type=jnp.float32
            )
            grad_keys = grad_keys + jnp.einsum(
                "hqk,qhd->khd", grad_scores, query_rows, preferred_element_type=jnp.float32
            )
            grad_values = grad_values + jnp.einsum(
                "hqk,qhd->khd",
                attn_probs.astype(jnp.bfloat16),
                grad_rows,
                preferred_element_type=jnp.float32,
            )
            return ((grad_keys, grad_values), grad_query)

        initial = (jnp.zeros(key_rows.shape, jnp.float32), jnp.zeros(value_rows.shape, jnp.float32))
        (grad_keys, grad_values), grad_queries = lax.scan(
            one_one_block, initial, jnp.arange(block_count)
        )
        return (grad_queries.reshape(key_rows.shape), grad_keys, grad_values)

    return lax.map(one_sequence, jnp.arange(seq_count))


def on_device(
    inputs,
    pass_ids,
    token_pos,
    pass_table,
    ln1_gain,
    ln1_bias,
    w_qkv,
    q_bias,
    v_bias,
    w_out,
    out_bias,
    ln2_gain,
    ln2_bias,
    w_up,
    up_bias,
    w_down,
    down_bias,
    cotangent,
):
    f32 = jnp.float32
    bf16 = jnp.bfloat16
    local_width = w_qkv.shape[2]
    head_size = D // HEADS
    heads_local = local_width // head_size
    seq_count, length = token_pos.shape
    total_rows = seq_count * length
    block_rows = min(512, length)
    seq_shape = (seq_count, length, heads_local, head_size)
    w_proj = w_qkv.reshape(D, 3 * local_width)
    onehot = (pass_ids[:, None] == jnp.arange(PASSES, dtype=jnp.int32)[None, :]).astype(f32)
    hidden = inputs.astype(f32) + jnp.dot(
        onehot, pass_table, precision=highest, preferred_element_type=f32
    )
    normed_f32, norm1_pull = jax.vjp(layer_norm, hidden, ln1_gain, ln1_bias)
    normed_all = lax.all_gather(normed_f32.astype(bf16), "tensor", axis=0, tiled=True)
    projected = jnp.dot(normed_all, w_proj, preferred_element_type=f32)
    queries = ((projected[:, :local_width] + q_bias) * 0.125).astype(bf16)
    key_all = projected[:, local_width : 2 * local_width].astype(bf16)
    value_all = (projected[:, 2 * local_width :] + v_bias).astype(bf16)
    query_seq = queries.reshape(seq_shape)
    key_seq = key_all.reshape(seq_shape)
    value_seq = value_all.reshape(seq_shape)
    contexts, log_totals = forward_attention(query_seq, key_seq, value_seq, token_pos, block_rows)
    context_low = contexts.reshape(total_rows, local_width).astype(bf16)
    rows_piece = context_low
    attn_share = lax.psum_scatter(
        jnp.dot(rows_piece, w_out, preferred_element_type=f32),
        "tensor",
        scatter_dimension=0,
        tiled=True,
    )
    resid = hidden + attn_share + out_bias
    normed2_f32, norm2_pull = jax.vjp(layer_norm, resid, ln2_gain, ln2_bias)
    mlp_in = lax.all_gather(normed2_f32.astype(bf16), "tensor", axis=0, tiled=True)
    pre_act = jnp.dot(mlp_in, w_up, preferred_element_type=f32) + up_bias
    activ_f32, gelu_pull = jax.vjp(gelu_tanh, pre_act)
    activ = activ_f32.astype(bf16)
    rows_piece = activ
    mlp_share = lax.psum_scatter(
        jnp.dot(rows_piece, w_down, preferred_element_type=f32).astype(jnp.bfloat16),
        "tensor",
        scatter_dimension=0,
        tiled=True,
    ).astype(jnp.float32)
    output = (resid + mlp_share + down_bias).astype(bf16)
    grad_out = cotangent.astype(f32)
    down_bias_part = jnp.sum(grad_out, axis=0)
    grad_mlp_all = lax.all_gather(cotangent, "tensor", axis=0, tiled=True)
    w_down_grad = contract_rows(activ, grad_mlp_all)
    grad_act = contract_cols(grad_mlp_all, w_down)
    grad_pre = gelu_pull(grad_act)[0].astype(bf16)
    up_bias_grad = jnp.sum(grad_pre.astype(f32), axis=0)
    w_up_grad = contract_rows(mlp_in, grad_pre)
    rows_piece = grad_pre
    grad_norm2 = lax.psum_scatter(
        contract_cols(rows_piece, w_up), "tensor", scatter_dimension=0, tiled=True
    )
    grad_resid_norm, ln2_gain_part, ln2_bias_part = norm2_pull(grad_norm2)
    grad_resid = grad_out + grad_resid_norm
    grad_attn = grad_resid.astype(bf16)
    out_bias_part = jnp.sum(grad_attn.astype(f32), axis=0)
    grad_attn_all = lax.all_gather(grad_attn, "tensor", axis=0, tiled=True)
    w_out_grad = contract_rows(context_low, grad_attn_all)
    grad_context = contract_cols(grad_attn_all, w_out).astype(bf16)
    grad_queries, grad_keys, grad_values = backward_attention(
        query_seq,
        key_seq,
        value_seq,
        grad_context.reshape(seq_shape),
        log_totals,
        token_pos,
        block_rows,
    )
    grad_query_low = grad_queries.reshape(total_rows, local_width).astype(bf16) * 0.125
    grad_key_low = grad_keys.reshape(total_rows, local_width).astype(bf16)
    grad_value_low = grad_values.reshape(total_rows, local_width).astype(bf16)
    grad_proj = jnp.concatenate([grad_query_low, grad_key_low, grad_value_low], axis=1)
    w_qkv_grad = contract_rows(normed_all, grad_proj).reshape(D, 3, local_width)
    q_bias_grad = jnp.sum(grad_query_low.astype(f32), axis=0)
    v_bias_grad = jnp.sum(grad_value_low.astype(f32), axis=0)
    rows_piece = grad_proj
    grad_norm1 = lax.psum_scatter(
        contract_cols(rows_piece, w_proj), "tensor", scatter_dimension=0, tiled=True
    )
    grad_hidden_norm, ln1_gain_part, ln1_bias_part = norm1_pull(grad_norm1)
    input_grad = grad_resid + grad_hidden_norm
    table_part = lax.dot_general(
        onehot, input_grad, (((0,), (0,)), ((), ())), precision=highest, preferred_element_type=f32
    )
    w_qkv_grad, q_bias_grad, v_bias_grad, w_out_grad, w_up_grad, up_bias_grad, w_down_grad = (
        lax.psum(
            (
                w_qkv_grad,
                q_bias_grad,
                v_bias_grad,
                w_out_grad,
                w_up_grad,
                up_bias_grad,
                w_down_grad,
            ),
            "dp",
        )
    )
    (
        table_grad,
        ln1_gain_grad,
        ln1_bias_grad,
        out_bias_grad,
        ln2_gain_grad,
        ln2_bias_grad,
        down_bias_grad,
    ) = lax.psum(
        (
            table_part,
            ln1_gain_part,
            ln1_bias_part,
            out_bias_part,
            ln2_gain_part,
            ln2_bias_part,
            down_bias_part,
        ),
        ("dp", "tensor"),
    )
    return (
        output,
        input_grad,
        table_grad,
        ln1_gain_grad,
        ln1_bias_grad,
        w_qkv_grad,
        q_bias_grad,
        v_bias_grad,
        w_out_grad,
        out_bias_grad,
        ln2_gain_grad,
        ln2_bias_grad,
        w_up_grad,
        up_bias_grad,
        w_down_grad,
        down_bias_grad,
    )


def solution(mesh):
    in_specs = (
        P(("dp", "tensor"), None),
        P(("dp", "tensor")),
        P("dp", None),
        P(),
        P(),
        P(),
        P(None, None, "tensor"),
        P("tensor"),
        P("tensor"),
        P("tensor", None),
        P(),
        P(),
        P(),
        P(None, "tensor"),
        P("tensor"),
        P("tensor", None),
        P(),
        P(("dp", "tensor"), None),
    )
    out_specs = (
        P(("dp", "tensor"), None),
        P(("dp", "tensor"), None),
        P(),
        P(),
        P(),
        P(None, None, "tensor"),
        P("tensor"),
        P("tensor"),
        P("tensor", None),
        P(),
        P(),
        P(),
        P(None, "tensor"),
        P("tensor"),
        P("tensor", None),
        P(),
    )
    return jax.shard_map(
        on_device, mesh=mesh, in_specs=in_specs, out_specs=out_specs, check_vma=False
    )
```

profile of v0, /device:TPU:0, one launch (start us, length us, event | category | flops | bytes accessed | tf_op | source)
XLA Modules:
  0.0 1087.9 jit_solution(9901813682815349103)
XLA Ops:
  11.1 66.3 %all-gather.5.cloned.1.call-done = bf16[2048,768]{1,0:T(8,128)(2,1)} async-done(((bf16[512,768]{1,0:T(8,128)(2,1)}), bf16[2048,768]{1,0:T(8,128)(2,1)}) %all-gather.5.cloned.1.call-update) | async-done | bytes 3145744 | tf_op jit(solution)/shard_map/all_gather | solution.py:156
  84.0 104.1 %while.40 = (s32[]{:T(128)}, bf16[4,512,3,64]{1,3,2,0:T(8,128)(2,1)}, f32[4,3,512,1]{2,1,3,0:T(4,128)}, s32[1,2048]{1,0:T(1,128)S(1)}, s32[4]{0:T(128)S(1)}, /*i...) while((s32[]{:T(128)}, ...), condition=%wide.region_5.6_spmd, body=%wide.region_2.5_spmd.sunk | while | flops 834664960 | bytes 53612952 | solution.py:64
  87.3 7.6 select_reduce_fusion.2
  94.8 7.9 fusion.115
  113.3 7.6 select_reduce_fusion.2
  120.9 7.9 fusion.115
  139.3 7.6 select_reduce_fusion.2
  146.9 7.9 fusion.115
  165.3 7.6 select_reduce_fusion.2
  172.9 7.9 fusion.115
  195.1 109.1 %reduce-scatter.5.cloned.1.call-done = f32[512,768]{1,0:T(8,128)} async-done(((f32[2048,768]{1,0:T(8,128)}), f32[512,768]{1,0:T(8,128)}) %reduce-scatter.5.cloned.1.call-update) | async-done | bytes 1572880 | tf_op jit(solution)/shard_map/reduce_scatter | solution.py:167
  309.0 63.5 %all-gather.7.cloned.1.call-done = bf16[2048,768]{1,0:T(8,128)(2,1)} async-done(((bf16[512,768]{1,0:T(8,128)(2,1)}), bf16[2048,768]{1,0:T(8,128)(2,1)}) %all-gather.7.cloned.1.call-update) | async-done | bytes 3145744 | tf_op jit(solution)/shard_map/all_gather | solution.py:175
  372.5 7.2 fusion.64
  379.7 56.4 %all-gather.9.cloned.1.call-done = bf16[2048,768]{1,0:T(8,128)(2,1)} async-done(((bf16[512,768]{1,0:T(8,128)(2,1)}), bf16[2048,768]{1,0:T(8,128)(2,1)}) %all-gather.9.cloned.1.call-update) | async-done | bytes 3145744 | tf_op jit(solution)/shard_map/all_gather | solution.py:189
  436.1 12.4 %convert_reduce_fusion = (f32[768]{0:T(1024)}, bf16[2048,768]{1,0:T(8,128)(2,1)S(1)}, bf16[2048,768]{1,0:T(8,128)(2,1)}) fusion(f32[2048,768]{1,0:T(8,128)} %fusion.64, f32[768]{0:T(1024)S(1)} %copy-done.61, bf16[2048,768]{1,0:T(8,128)(2,1)} %all-gather.9.cloned.1.call-done, bf16[768,768]{1,0:T(8,128)(2,1)S(1)} %copy-done), kind=kOutput, calls=%fused_computation.53 | convolution fusion | flops 2455239936 | bytes 16914432 | tf_op jit(solution)/shard_map/dot_general | solution.py:32
  461.2 103.1 %reduce-scatter.9.cloned.1.call-done = f32[512,768]{1,0:T(8,128)} async-done(((f32[2048,768]{1,0:T(8,128)}), f32[512,768]{1,0:T(8,128)}) %reduce-scatter.9.cloned.1.call-update) | async-done | bytes 1572880 | tf_op jit(solution)/shard_map/reduce_scatter | solution.py:196
  567.0 60.3 %reduce-scatter.7.cloned.1.call-done = bf16[512,768]{1,0:T(8,128)(2,1)} async-done(((bf16[2048,768]{1,0:T(8,128)(2,1)}), bf16[512,768]{1,0:T(8,128)(2,1)}) %reduce-scatter.7.cloned.1.call-update) | async-done | bytes 786448 | tf_op jit(solution)/shard_map/reduce_scatter | solution.py:180
  633.6 63.6 %all-gather.11.cloned.1.call-done = bf16[2048,768]{1,0:T(8,128)(2,1)} async-done(((bf16[512,768]{1,0:T(8,128)(2,1)}), bf16[2048,768]{1,0:T(8,128)(2,1)}) %all-gather.11.cloned.1.call-update) | async-done | bytes 3145744 | tf_op jit(solution)/shard_map/all_gather | solution.py:203
  701.2 134.3 %while.41 = (s32[]{:T(128)}, f32[2048,3,64]{0,2,1:T(8,128)}, f32[2048,3,64]{0,2,1:T(8,128)}, bf16[4,512,3,64]{1,3,2,0:T(8,128)(2,1)}, s32[4]{0:T(128)S(1)}, /*in...) while((s32[]{:T(128)}, f32[2048,3,64]{0,2,1:T(8,128)}, ...), condition=%wide.region_15.16_spmd.clone, body=%wide.region_13.15_spmd.clone.sunk | while | flops 2053634560 | bytes 150399440 | solution.py:113
  844.3 7.1 fusion.68
  861.6 15.1 %all-reduce.1 = (f32[192]{0:T(256)}, f32[192]{0:T(256)}, f32[768]{0:T(1024)}) all-reduce(f32[192]{0:T(256)S(1)} %reduce_sum.221, f32[192]{0:T(256)S(1)} %reduce_sum.223, f32[768]{0:T(1024)S(1)} %copy-done.54), channel_id=1, replica_groups=mesh['dp'=8,'tensor'=4] {'dp'}, use_global_device_ids=true, to_apply=%region_26.27 | all-reduce | flops 1152 | bytes 9216 | tf_op jit(solution)/shard_map/psum | solution.py:232
  876.8 77.0 %reduce-scatter.11.cloned.1.call-done = f32[512,768]{1,0:T(8,128)} async-done(((f32[2048,768]{1,0:T(8,128)}), f32[512,768]{1,0:T(8,128)}) %reduce-scatter.11.cloned.1.call-update) | async-done | bytes 1572880 | tf_op jit(solution)/shard_map/reduce_scatter | solution.py:223
  959.0 42.7 %all-reduce = (f32[5,768]{1,0:T(8,128)}, f32[768]{0:T(1024)}, f32[768]{0:T(1024)}, f32[768]{0:T(1024)}, f32[768]{0:T(1024)}, /*index=5*/f32[768]{0:T(1024)}, f32[768]{0:T(1024)}) all-reduce(f32[5,768]{1,0:T(8,128)S(1)} %fusion.49, f32[768]{0:T(1024)S(1)} %get-tuple-element.251, ...), channel_id=1, replica_groups=mesh['dp'=8,'tensor'=4] {'dp','tensor'}, use_global_device_ids=true, to_apply=%region_19.20 | all-reduce | flops 8448 | bytes 67584 | tf_op jit(solution)/shard_map/psum | solution.py:253
  1001.7 71.5 %all-reduce.5.cloned.1.call-done = (f32[768,3,192]{0,2,1:T(8,128)}, f32[192,768]{1,0:T(8,128)}, f32[768,768]{1,0:T(8,128)}, f32[768,768]{1,0:T(8,128)}) async-done(((f32[768,3,192]{0,2,1:T(8,128)}, f32[192,768]{1,0:T(8,128)}, f32[768,768]{1,0:T(8,128)}, f32[768,768]{1,0:T(8,128)}), (f32[768,3,192]{0,2,1:T(8,128)}, f32[192,768]{1,0:T(8,128)}, f32[768,768]{1,0:T(8,128)}, ...) | async-done | bytes 7077904 | tf_op jit(solution)/shard_map/psum | solution.py:232
  (312 shorter events, 236.7 us)
Async XLA Ops:
  7.2 428.9 %copy-start = (bf16[768,768]{1,0:T(8,128)(2,1)S(1)}, bf16[768,768]{1,0:T(8,128)(2,1)}, u32[]{:S(2)}) copy-start(bf16[768,768]{1,0:T(8,128)(2,1)} %param.37) | copy-start | bytes 3538948
  7.2 70.2 %all-gather.5.cloned.1.call-start = ((), (), s32[]{:S(2)}) async-start(), calls=%async_computation.4 | async-start | bytes 3932160 | tf_op jit(solution)/shard_map/all_gather | solution.py:156
  9.4 294.8 %copy-start.7 = (f32[512,768]{1,0:T(8,128)}, f32[512,768]{1,0:T(8,128)S(1)}, u32[]{:S(2)}) copy-start(f32[512,768]{1,0:T(8,128)S(1)} %get-tuple-element.332) | copy-start | bytes 4718596
  11.1 293.2 %reduce-scatter.5.cloned.1.call-start = ((), (), s32[]{:S(2)}) async-start(), calls=%async_computation.5 | async-start | bytes 7864320 | tf_op jit(solution)/shard_map/reduce_scatter | solution.py:167
  194.7 109.6 %copy-start.51 = (f32[768]{0:T(1024)S(1)}, f32[768]{0:T(1024)}, u32[]{:S(2)}) copy-start(f32[768]{0:T(1024)} %param.32) | copy-start | bytes 9220
  194.7 112.4 %copy-start.33 = (f32[768]{0:T(1024)S(1)}, f32[768]{0:T(1024)}, u32[]{:S(2)}) copy-start(f32[768]{0:T(1024)} %param.33) | copy-start | bytes 9220
  194.7 177.8 %all-gather.7.cloned.1.call-start = ((), (), s32[]{:S(2)}) async-start(), calls=%async_computation.6 | async-start | bytes 3932160 | tf_op jit(solution)/shard_map/all_gather | solution.py:175
  308.3 127.8 %all-gather.9.cloned.1.call-start = ((), (), s32[]{:S(2)}) async-start(), calls=%async_computation.8 | async-start | bytes 3932160 | tf_op jit(solution)/shard_map/all_gather | solution.py:189
  308.9 127.2 %copy-start.61 = (f32[768]{0:T(1024)S(1)}, f32[768]{0:T(1024)}, u32[]{:S(2)}) copy-start(f32[768]{0:T(1024)} %param.36) | copy-start | bytes 9220
  308.9 255.4 %reduce-scatter.9.cloned.1.call-start = ((), (), s32[]{:S(2)}) async-start(), calls=%async_computation.9 | async-start | bytes 7864320 | tf_op jit(solution)/shard_map/reduce_scatter | solution.py:196
  454.8 172.5 %reduce-scatter.7.cloned.1.call-start = ((), (), s32[]{:S(2)}) async-start(), calls=%async_computation.7 | async-start | bytes 3932160 | tf_op jit(solution)/shard_map/reduce_scatter | solution.py:180
  461.1 103.2 %copy-start.11 = (f32[512,768]{1,0:T(8,128)S(1)}, f32[512,768]{1,0:T(8,128)}, u32[]{:S(2)}) copy-start(f32[512,768]{1,0:T(8,128)} %copy-done.10) | copy-start | bytes 4718596
  461.1 103.2 %copy-start.39 = (f32[512]{0:T(512)S(1)}, f32[512]{0:T(512)}, u32[]{:S(2)}) copy-start(f32[512]{0:T(512)} %copy-done.38) | copy-start | bytes 6148
  461.1 105.8 %copy-start.43 = (f32[512]{0:T(512)S(1)}, f32[512]{0:T(512)}, u32[]{:S(2)}) copy-start(f32[512]{0:T(512)} %copy-done.42) | copy-start | bytes 6148
  461.1 166.2 %copy-start.53 = (f32[768]{0:T(1024)S(1)}, f32[768]{0:T(1024)}, u32[]{:S(2)}) copy-start(f32[768]{0:T(1024)} %param.38) | copy-start | bytes 9220
  461.1 236.0 %all-gather.11.cloned.1.call-start = ((), (), s32[]{:S(2)}) async-start(), calls=%async_computation.10 | async-start | bytes 3932160 | tf_op jit(solution)/shard_map/all_gather | solution.py:203
  633.5 320.3 %reduce-scatter.11.cloned.1.call-start = ((), (), s32[]{:S(2)}) async-start(), calls=%async_computation.11 | async-start | bytes 7864320 | tf_op jit(solution)/shard_map/reduce_scatter | solution.py:223
  844.2 229.0 %all-reduce.5.cloned.1.call-start = ((), (), s32[]{:S(2)}) async-start(), calls=%async_computation.12 | async-start | bytes 14155776 | tf_op jit(solution)/shard_map/psum | solution.py:232
  860.9 92.9 %copy-start.8 = (f32[512,768]{1,0:T(8,128)S(1)}, f32[512,768]{1,0:T(8,128)}, u32[]{:S(2)}) copy-start(f32[512,768]{1,0:T(8,128)} %copy-done.7) | copy-start | bytes 4718596
  860.9 92.9 %copy-start.32 = (f32[512]{0:T(512)S(1)}, f32[512]{0:T(512)}, u32[]{:S(2)}) copy-start(f32[512]{0:T(512)} %copy-done.31) | copy-start | bytes 6148
  860.9 92.9 %copy-start.35 = (f32[768]{0:T(1024)S(1)}, f32[768]{0:T(1024)}, u32[]{:S(2)}) copy-start(f32[768]{0:T(1024)} %param.26) | copy-start | bytes 9220
  860.9 92.9 %copy-start.37 = (f32[512]{0:T(512)S(1)}, f32[512]{0:T(512)}, u32[]{:S(2)}) copy-start(f32[512]{0:T(512)} %copy-done.36) | copy-start | bytes 6148
  861.0 95.0 %copy-start.41 = (f32[512]{0:T(512)S(1)}, f32[512]{0:T(512)}, u32[]{:S(2)}) copy-start(f32[512]{0:T(512)} %copy-done.40) | copy-start | bytes 6148
  958.0 118.1 %copy-start.18 = (f32[512,768]{1,0:T(8,128)}, f32[512,768]{1,0:T(8,128)S(1)}, u32[]{:S(2)}) copy-start(f32[512,768]{1,0:T(8,128)S(1)} %get-tuple-element.548) | copy-start | bytes 4718596
  (76 other events, 826.0 us)
Sparse Core Ops, SparseCore 0:
  11.2 66.1 all-gather.4
  194.8 109.3 reduce-scatter.4
  308.4 64.0 all-gather.6
  373.9 62.1 all-gather.8
  454.9 109.3 reduce-scatter.8
  566.5 60.7 reduce-scatter.6
  633.6 63.5 all-gather.10
  844.4 109.3 reduce-scatter.10
  958.6 114.5 all-reduce.4
where the time goes:
time: 1100 us; the launch traced here: 1090 us
  waiting for transfers between devices  672 us (61%)
  matrix products  212 us (19%)
  other arithmetic  83 us (8%)
  blocking collectives  57.8 us (5%)
  local copies, waits for them, and re-layouts  28.6 us (3%)
  loops' own time  19 us (2%)
  between operations  14.8 us (1%)
    reduce_scatter x1, waiting for transfers between devices, on_device(): lax.psum_scatter(jnp.dot(rows_piece, w_out, preferred_element_type=f32),...  109 us
    reduce_scatter x1, waiting for transfers between devices, on_device(): lax.psum_scatter(contract_cols(rows_piece, w_up), 'tensor', scatter_dimen...  103 us
    reduce_scatter x1, waiting for transfers between devices, on_device(): lax.psum_scatter(contract_cols(rows_piece, w_proj), 'tensor', scatter_dim...  77 us
    psum x1, waiting for transfers between devices, on_device(): lax.psum((w_qkv_grad, q_bias_grad, v_bias_grad, w_out_grad, w_up_grad, up...  71.5 us
    all_gather x1, waiting for transfers between devices, on_device(): lax.all_gather(normed_f32.astype(bf16), 'tensor', axis=0, tiled=True)  66.3 us
    all_gather x1, waiting for transfers between devices, on_device(): grad_attn_all = lax.all_gather(grad_attn, 'tensor', axis=0, tiled=True)  63.6 us
    all_gather x1, waiting for transfers between devices, on_device(): lax.all_gather(normed2_f32.astype(bf16), 'tensor', axis=0, tiled=True)  63.5 us
    reduce_scatter x1, waiting for transfers between devices, on_device(): lax.psum_scatter(jnp.dot(rows_piece, w_down, preferred_element_type=f32)....  60.3 us
  transfers between devices with their start and end apart: 9, of which 9 were waited for; matrix products, arithmetic and copies ran while one was open for 3% of the time, Pallas kernels for 0%

commit v1 on v0

v1 whole, which is shorter than its diff:
```python
import functools

import jax
import jax.numpy as jnp
from jax import lax
from jax.experimental import pallas as pl
from jax.experimental.pallas import tpu as pltpu
from jax.sharding import PartitionSpec as P

D = 768
HEADS = 12
HD = D // HEADS
PASSES = 5
EPS = 1e-05
NEG = -1e30
TIES = 128

f32 = jnp.float32
bf16 = jnp.bfloat16
MESH = pl.DeviceIdType.MESH


def dot_nn(a, b):
    return lax.dot_general(a, b, (((1,), (0,)), ((), ())), preferred_element_type=f32)


def dot_nt(a, b):
    return lax.dot_general(a, b, (((1,), (1,)), ((), ())), preferred_element_type=f32)


def dot_tn(a, b):
    return lax.dot_general(a, b, (((0,), (0,)), ((), ())), preferred_element_type=f32)


def head_lanes(h, rows, width):
    lane = lax.broadcasted_iota(jnp.int32, (rows, width), 1)
    return (lane >= h * HD) & (lane < (h + 1) * HD)


def only_head(h, rows):
    return jnp.where(head_lanes(h, *rows.shape), rows, jnp.zeros((), rows.dtype))


def attn_fwd_kernel(
    BQ, x_ref, wq_ref, wk_ref, wv_ref, qb_ref, vb_ref, posr_ref, posc_ref,
    ctx_ref, lse_ref, q_ref, k_ref, v_ref,
):
    length, width = ctx_ref.shape
    heads = width // HD

    def project(i, carry):
        r = pl.ds(pl.multiple_of(i * BQ, BQ), BQ)
        x = x_ref[r, :]
        q_ref[r, :] = ((dot_nn(x, wq_ref[...]) + qb_ref[...]) * 0.125).astype(bf16)
        k_ref[r, :] = dot_nn(x, wk_ref[...]).astype(bf16)
        v_ref[r, :] = (dot_nn(x, wv_ref[...]) + vb_ref[...]).astype(bf16)
        return carry

    lax.fori_loop(0, length // BQ, project, 0)

    def one_head(h, carry):
        for i in range(length // BQ):
            r0, r1 = i * BQ, (i + 1) * BQ
            hi = min(length, r1 + TIES)
            mine = head_lanes(h, BQ, width)
            q = jnp.where(mine, q_ref[r0:r1, :], jnp.zeros((), bf16))
            s1 = dot_nt(q, k_ref[r0:hi, :])
            s1 = jnp.where(posr_ref[:, r0:hi] <= posc_ref[r0:r1, :], s1, NEG)
            m = jnp.max(s1, axis=1, keepdims=True)
            if i:
                s0 = dot_nt(q, k_ref[0:r0, :])
                m = jnp.maximum(m, jnp.max(s0, axis=1, keepdims=True))
            p1 = jnp.exp(s1 - m)
            total = jnp.sum(p1, axis=1, keepdims=True)
            acc = dot_nn(p1.astype(bf16), v_ref[r0:hi, :])
            if i:
                p0 = jnp.exp(s0 - m)
                total = total + jnp.sum(p0, axis=1, keepdims=True)
                acc = acc + dot_nn(p0.astype(bf16), v_ref[0:r0, :])
            out = (acc / total).astype(bf16)
            ctx_ref[r0:r1, :] = jnp.where(mine, out, ctx_ref[r0:r1, :])
            lse_ref[pl.ds(h, 1), r0:r1] = jnp.reshape(m + jnp.log(total), (1, BQ))
        return carry

    ctx_ref[...] = jnp.zeros_like(ctx_ref)
    lax.fori_loop(0, heads, one_head, 0)


def attn_bwd_kernel(
    BQ, q_ref, k_ref, v_ref, g_ref, ctx_ref, posr_ref, posc_ref, lse_ref,
    dq_ref, dk_ref, dv_ref, dka, dva,
):
    length, width = q_ref.shape
    heads = width // HD
    dka[...] = jnp.zeros_like(dka)
    dva[...] = jnp.zeros_like(dva)
    pick = (
        lax.broadcasted_iota(jnp.int32, (8, width), 1) // HD
        == lax.broadcasted_iota(jnp.int32, (8, width), 0)
    ).astype(f32)
    for i in range(length // BQ):
        r0, r1 = i * BQ, (i + 1) * BQ
        hi = min(length, r1 + TIES)
        posr = posr_ref[:, r0:r1]
        g_all, q_all = g_ref[r0:r1, :], q_ref[r0:r1, :]
        prod = g_all.astype(f32) * ctx_ref[r0:r1, :].astype(f32)
        delta = lax.dot_general(
            pick, prod, (((1,), (1,)), ((), ())),
            precision=lax.Precision.HIGHEST, preferred_element_type=f32,
        )
        qs = [only_head(h, q_all) for h in range(heads)]
        gs = [only_head(h, g_all) for h in range(heads)]
        qc, gc = jnp.concatenate(qs, axis=0), jnp.concatenate(gs, axis=0)
        dq = [None] * heads
        for a, b, masked in ([(0, r0, False)] if i else []) + [(r0, hi, True)]:
            ps, dss = [], []
            for h in range(heads):
                st = dot_nt(k_ref[a:b, :], qs[h])
                p = jnp.exp(st - lse_ref[h : h + 1, r0:r1])
                if masked:
                    p = jnp.where(posc_ref[a:b, :] <= posr, p, 0.0)
                dp = dot_nt(v_ref[a:b, :], gs[h])
                ds = (p * (dp - delta[h : h + 1, :])).astype(bf16)
                ps.append(p.astype(bf16))
                dss.append(ds)
                t = dot_tn(ds, k_ref[a:b, :])
                dq[h] = t if dq[h] is None else dq[h] + t
            dva[a:b, :] += dot_nn(jnp.concatenate(ps, axis=1), gc)
            dka[a:b, :] += dot_nn(jnp.concatenate(dss, axis=1), qc)
        out = dq[0]
        for h in range(1, heads):
            out = jnp.where(head_lanes(h, BQ, width), dq[h], out)
        dq_ref[r0:r1, :] = out.astype(bf16) * jnp.asarray(0.125, bf16)
    dk_ref[...] = dka[...].astype(bf16)
    dv_ref[...] = dva[...].astype(bf16)


def in_vmem(n):
    return [pl.BlockSpec(memory_space=pltpu.VMEM)] * n


def attention_forward(x, wq, wk, wv, qb, vb, posr, posc, block):
    length, width = x.shape[0], wq.shape[1]
    s = jax.ShapeDtypeStruct
    area = length * length * width
    return pl.pallas_call(
        functools.partial(attn_fwd_kernel, block),
        out_shape=(
            s((length, width), bf16), s((width // HD, length), f32),
            s((length, width), bf16), s((length, width), bf16), s((length, width), bf16),
        ),
        in_specs=in_vmem(8),
        out_specs=tuple(in_vmem(5)),
        compiler_params=pltpu.CompilerParams(vmem_limit_bytes=56 << 20),
        cost_estimate=pl.CostEstimate(
            flops=12 * area, bytes_accessed=8 << 20, transcendentals=length * length * 2
        ),
        name="attn_fwd",
    )(x, wq, wk, wv, qb, vb, posr, posc)


def attention_backward(q, k, v, g, ctx, posr, posc, lse, block):
    length, width = q.shape
    s = jax.ShapeDtypeStruct
    area = length * length * width
    return pl.pallas_call(
        functools.partial(attn_bwd_kernel, block),
        out_shape=(s((length, width), bf16),) * 3,
        in_specs=in_vmem(8),
        out_specs=tuple(in_vmem(3)),
        scratch_shapes=[pltpu.VMEM((length, width), f32), pltpu.VMEM((length, width), f32)],
        compiler_params=pltpu.CompilerParams(vmem_limit_bytes=56 << 20),
        cost_estimate=pl.CostEstimate(
            flops=20 * area, bytes_accessed=8 << 20, transcendentals=length * length * 2
        ),
        name="attn_bwd",
    )(q, k, v, g, ctx, posr, posc, lse)


def swap_kernel(n, x_ref, o_ref, own_sem, send_sem, recv_sem):
    me = lax.axis_index("tensor")
    dp = lax.axis_index("dp")
    peers = [lax.rem(me + k, n) for k in range(1, n)]
    barrier = pltpu.get_barrier_semaphore()
    for peer in peers:
        pl.semaphore_signal(barrier, inc=1, device_id=(dp, peer), device_id_type=MESH)
    pl.semaphore_wait(barrier, n - 1)
    own = pltpu.make_async_copy(x_ref.at[me], o_ref.at[me], own_sem)
    copies = [
        pltpu.make_async_remote_copy(
            src_ref=x_ref.at[peer], dst_ref=o_ref.at[me],
            send_sem=send_sem.at[k], recv_sem=recv_sem.at[k],
            device_id=(dp, peer), device_id_type=MESH,
        )
        for k, peer in enumerate(peers)
    ]
    for copy in copies:
        copy.start()
    own.start()
    own.wait()
    for copy in copies:
        copy.wait()


def swap(x, collective_id):
    n = x.shape[0]
    return pl.pallas_call(
        functools.partial(swap_kernel, n),
        out_shape=jax.ShapeDtypeStruct(x.shape, x.dtype),
        in_specs=[pl.BlockSpec(memory_space=pl.ANY)],
        out_specs=pl.BlockSpec(memory_space=pl.ANY),
        scratch_shapes=[
            pltpu.SemaphoreType.DMA, pltpu.SemaphoreType.DMA((n - 1,)),
            pltpu.SemaphoreType.DMA((n - 1,)),
        ],
        compiler_params=pltpu.CompilerParams(collective_id=collective_id, has_side_effects=True),
        cost_estimate=pl.CostEstimate(flops=0, bytes_accessed=32 << 20, transcendentals=0),
        name=f"swap{collective_id}",
    )(x)


def norm_stats(values):
    centered = values - jnp.mean(values, axis=-1, keepdims=True)
    inv = lax.rsqrt(jnp.mean(centered * centered, axis=-1, keepdims=True) + EPS)
    return centered * inv, inv


def norm_back(grad, n, inv, gain):
    e = grad * gain
    dv = inv * (
        e - jnp.mean(e, axis=-1, keepdims=True) - n * jnp.mean(e * n, axis=-1, keepdims=True)
    )
    return dv, jnp.sum(grad * n, axis=0), jnp.sum(grad, axis=0)


def gelu_parts(u):
    c = 0.7978845608028654
    t = jnp.tanh(c * (u + 0.044715 * u * u * u))
    act = 0.5 * u * (1.0 + t)
    slope = 0.5 * (1.0 + t) + 0.5 * u * (1.0 - t * t) * c * (1.0 + 3 * 0.044715 * u * u)
    return act, slope


def on_device(
    inputs, pass_ids, token_pos, pass_table, ln1_gain, ln1_bias, w_qkv, q_bias, v_bias, w_out,
    out_bias, ln2_gain, ln2_bias, w_up, up_bias, w_down, down_bias, cotangent, *, nt, nd,
):
    width = w_qkv.shape[2]
    length = token_pos.shape[1]
    rows = inputs.shape[0]
    hid = w_up.shape[1]
    everyone = ("tensor", "dp")
    dpi = lax.axis_index("dp")

    onehot = (pass_ids[:, None] == jnp.arange(PASSES, dtype=jnp.int32)[None, :]).astype(f32)
    hidden = inputs.astype(f32)
    for p in range(PASSES):
        hidden = hidden + jnp.where((pass_ids == p)[:, None], pass_table[p][None, :], 0.0)
    n1, inv1 = norm_stats(hidden)
    normed = (n1 * ln1_gain + ln1_bias).astype(bf16)
    normed_all = lax.all_gather(normed, "tensor", axis=0, tiled=True)

    def whole(w):
        part = w.shape[0] // nd
        mine = lax.dynamic_slice_in_dim(w, dpi * part, part, 0)
        return lax.all_gather(mine, everyone, axis=0, tiled=True)

    w_out_all = whole(w_out)
    w_up_all = whole(w_up).reshape(nt, D, hid)
    w_down_all = whole(w_down)
    up_bias_all = lax.all_gather(up_bias, "tensor", axis=0, tiled=True)

    posr, posc = token_pos.reshape(1, length), token_pos.reshape(length, 1)
    wq, wk, wv = w_qkv[:, 0, :], w_qkv[:, 1, :], w_qkv[:, 2, :]
    ctx, lse, q, k, v = attention_forward(
        normed_all, wq, wk, wv, q_bias[None, :], v_bias[None, :], posr, posc, 256
    )
    mine = swap(ctx.reshape(nt, rows, width), 1)
    context = jnp.transpose(mine, (1, 0, 2)).reshape(rows, D)

    resid = hidden + dot_nn(context, w_out_all) + out_bias
    n2, inv2 = norm_stats(resid)
    normed2 = (n2 * ln2_gain + ln2_bias).astype(bf16)
    acts, slopes = [], []
    for z in range(nt):
        u = dot_nn(normed2, w_up_all[z]) + up_bias_all[z * hid : (z + 1) * hid]
        a, s = gelu_parts(u)
        acts.append(a.astype(bf16))
        slopes.append(s)
    activ = jnp.concatenate(acts, axis=1)
    slope = jnp.concatenate(slopes, axis=1)
    output = (resid + dot_nn(activ, w_down_all) + down_bias).astype(bf16)
    grad_out = cotangent.astype(f32)
    down_bias_part = jnp.sum(grad_out, axis=0)
    w_down_part = dot_tn(activ, cotangent)
    grad_pre = (dot_nt(cotangent, w_down_all) * slope).astype(bf16)
    up_bias_part = jnp.sum(grad_pre.astype(f32), axis=0)
    w_up_parts = [dot_tn(normed2, grad_pre[:, z * hid : (z + 1) * hid]) for z in range(nt)]
    w_up_part = jnp.concatenate(w_up_parts, axis=0)
    grad_norm2 = jnp.zeros((rows, D), f32)
    for z in range(nt):
        grad_norm2 = grad_norm2 + dot_nt(grad_pre[:, z * hid : (z + 1) * hid], w_up_all[z])
    back2, ln2_gain_part, ln2_bias_part = norm_back(grad_norm2, n2, inv2, ln2_gain)
    grad_resid = grad_out + back2
    grad_attn = grad_resid.astype(bf16)
    out_bias_part = jnp.sum(grad_attn.astype(f32), axis=0)
    w_out_part = dot_tn(context, grad_attn)
    grad_context = dot_nt(grad_attn, w_out_all).astype(bf16)
    send = jnp.transpose(grad_context.reshape(rows, nt, width), (1, 0, 2))
    g = swap(send, 2).reshape(length, width)

    def reduced(part):
        shard = lax.psum_scatter(
            part.astype(bf16), everyone, scatter_dimension=0, tiled=True
        )
        return lax.all_gather(shard, "dp", axis=0, tiled=True).astype(f32)

    w_down_grad = reduced(w_down_part)
    w_up_grad = reduced(w_up_part)
    w_out_grad = reduced(w_out_part)

    dq, dk, dv = attention_backward(q, k, v, g, ctx, posr, posc, lse, 256)
    share = dot_nt(dq, wq) + dot_nt(dk, wk) + dot_nt(dv, wv)
    grad_norm1 = lax.psum_scatter(
        share.astype(bf16), "tensor", scatter_dimension=0, tiled=True
    ).astype(f32)
    w_qkv_grad = jnp.stack([dot_tn(normed_all, t) for t in (dq, dk, dv)], axis=1)
    q_bias_grad = jnp.sum(dq.astype(f32), axis=0)
    v_bias_grad = jnp.sum(dv.astype(f32), axis=0)
    back1, ln1_gain_part, ln1_bias_part = norm_back(grad_norm1, n1, inv1, ln1_gain)
    input_grad = grad_resid + back1
    table_part = lax.dot_general(
        onehot, input_grad, (((0,), (0,)), ((), ())),
        precision=lax.Precision.HIGHEST, preferred_element_type=f32,
    )
    w_qkv_grad, q_bias_grad, v_bias_grad = lax.psum((w_qkv_grad, q_bias_grad, v_bias_grad), "dp")
    (
        table_grad, ln1_gain_grad, ln1_bias_grad, out_bias_grad, ln2_gain_grad, ln2_bias_grad,
        down_bias_grad, up_bias_all_grad,
    ) = lax.psum(
        (
            table_part, ln1_gain_part, ln1_bias_part, out_bias_part, ln2_gain_part, ln2_bias_part,
            down_bias_part, up_bias_part,
        ),
        ("dp", "tensor"),
    )
    up_bias_grad = lax.dynamic_slice_in_dim(
        up_bias_all_grad, lax.axis_index("tensor") * hid, hid, 0
    )
    return (
        output, input_grad, table_grad, ln1_gain_grad, ln1_bias_grad, w_qkv_grad, q_bias_grad,
        v_bias_grad, w_out_grad, out_bias_grad, ln2_gain_grad, ln2_bias_grad, w_up_grad,
        up_bias_grad, w_down_grad, down_bias_grad,
    )


def solution(mesh):
    both = ("dp", "tensor")
    in_specs = (
        P(both, None), P(both), P("dp", None), P(), P(), P(), P(None, None, "tensor"),
        P("tensor"), P("tensor"), P("tensor", None), P(), P(), P(), P(None, "tensor"),
        P("tensor"), P("tensor", None), P(), P(both, None),
    )
    out_specs = (
        P(both, None), P(both, None), P(), P(), P(), P(None, None, "tensor"), P("tensor"),
        P("tensor"), P("tensor", None), P(), P(), P(), P(None, "tensor"), P("tensor"),
        P("tensor", None), P(),
    )
    body = functools.partial(on_device, nt=mesh.shape["tensor"], nd=mesh.shape["dp"])
    return jax.shard_map(
        body, mesh=mesh, in_specs=in_specs, out_specs=out_specs, check_vma=False
    )
```

time: 1100 us -> 802 us (0.73)
  waiting for transfers between devices: 672 us -> 490 us
  matrix products: 212 us -> 65.6 us
  Pallas kernels: 0 us -> 100 us
  other arithmetic: 83 us -> 20.6 us
  blocking collectives: 57.8 us -> 78.6 us
  loops' own time: 19 us -> 0 us
    dot_general x42 -> x25, matrix products: 212 us -> 65.6 us  [the longest x9 23.6 us: dot_nt(): lax.dot_general(a, b, (((1,), (1,)), ((), ())), preferred_element_type=f32)]
    pallas_call x0 -> x4, Pallas kernels: none -> 100 us  [the longest x2 45.3 us: swap(): pl.pallas_call(functools.partial(swap_kernel, n), out_shape=jax.ShapeDtyp...]
    reduce_scatter x4, waiting for transfers between devices: 350 us -> 256 us  [the longest x3 205 us: reduced(): lax.psum_scatter(part.astype(bf16), everyone, scatter_dimension=0, tiled=...]
    all_gather x4 -> x6, waiting for transfers between devices: 250 us -> 173 us  [the longest x3 130 us: whole(): return lax.all_gather(mine, everyone, axis=0, tiled=True)]
    reduce_sum x14 -> x6, other arithmetic: 45.9 us -> 5.23 us  [the longest x1 2.1 us: norm_stats(): centered = values - jnp.mean(values, axis=-1, keepdims=True)]
    all_gather x0 -> x2, blocking collectives: none -> 24.4 us  [the longest x1 14.9 us: on_device(): up_bias_all = lax.all_gather(up_bias, 'tensor', axis=0, tiled=True)]
    convert_element_type x8 -> x5, other arithmetic: 27.3 us -> 8.06 us  [the longest x3 6.55 us: reduced(): return lax.all_gather(shard, 'dp', axis=0, tiled=True).astype(f32)]
    another operation x2 -> x0, loops' own time: 19 us -> none  [the longest x1 11 us: one_sequence(): lax.scan(one_one_block, initial, jnp.arange(block_count))]
  transfers between devices with their start and end apart: 9 -> 11, of which waited for: 9 -> 10; matrix products, arithmetic and copies ran while one was open for 3% -> 11% of each run, Pallas kernels for 0% -> 13%
where the time goes in v1:
time: 802 us; the launch traced here: 795 us
  waiting for transfers between devices  490 us (61%)
  Pallas kernels  100 us (12%)
  blocking collectives  78.6 us (10%)
  matrix products  65.6 us (8%)
  local copies, waits for them, and re-layouts  24.4 us (3%)
  other arithmetic  20.6 us (3%)
  between operations  14.5 us (2%)
    reduce_scatter x3, waiting for transfers between devices, reduced(): lax.psum_scatter(part.astype(bf16), everyone, scatter_dimension=0, tiled=...  205 us
    all_gather x3, waiting for transfers between devices, whole(): return lax.all_gather(mine, everyone, axis=0, tiled=True)  130 us
    psum x1, waiting for transfers between devices, on_device(): lax.psum((w_qkv_grad, q_bias_grad, v_bias_grad), 'dp')  61 us
    reduce_scatter x1, waiting for transfers between devices, on_device(): lax.psum_scatter(share.astype(bf16), 'tensor', scatter_dimension=0, tiled...  51.3 us
    pallas_call x2, Pallas kernels, swap(): pl.pallas_call(functools.partial(swap_kernel, n), out_shape=jax.ShapeDtyp...  45.3 us
    all_gather x1, waiting for transfers between devices, on_device(): normed_all = lax.all_gather(normed, 'tensor', axis=0, tiled=True)  42.3 us
    psum x1, blocking collectives, on_device(): lax.psum((table_part, ln1_gain_part, ln1_bias_part, out_bias_part, ln2_ga...  41.8 us
    pallas_call x1, Pallas kernels, attention_backward(): pl.pallas_call(functools.partial(attn_bwd_kernel, block), out_shape=(s((l...  30.6 us
  transfers between devices with their start and end apart: 11, of which 10 were waited for; matrix products, arithmetic and copies ran while one was open for 11% of the time, Pallas kernels for 13%

profile of v1, /device:TPU:0, one launch (start us, length us, event | category | flops | bytes accessed | tf_op | source)
XLA Modules:
  0.0 795.1 jit_solution(3533250800897941190)
XLA Ops:
  22.0 14.9 %all-gather = f32[4,1,768]{2,1,0:T(1,128)S(1)} all-gather(f32[1,1,768]{2,1,0:T(1,128)S(1)} %reshape.117), channel_id=1, replica_groups=mesh['dp'=8,'tensor'=4] {'tensor'}, dimensions={0}, use_global_device_ids=true | all-gather | bytes 15360 | tf_op jit(solution)/shard_map/all_gather | solution.py:271
  36.9 42.3 %all-gather.8.cloned.1.call-done.x_ref = bf16[2048,768]{1,0:T(8,128)(2,1)} async-done(((bf16[512,768]{1,0:T(8,128)(2,1)}), bf16[2048,768]{1,0:T(8,128)(2,1)}) %all-gather.8.cloned.1.call-update) | async-done | bytes 3145744 | tf_op jit(solution)/shard_map/all_gather | solution.py:261
  79.2 24.4 %attn_fwd.1 = (bf16[2048,192]{1,0:T(8,128)(2,1)}, f32[3,2048]{1,0:T(4,128)}, bf16[2048,192]{1,0:T(8,128)(2,1)}, bf16[2048,192]{1,0:T(8,128)(2,1)}, bf16[2048,192]{1,0:T(8,128)(2,1)}) custom-call(bf16[2048,768]{1,0:T(8,128)(2,1)} %all-gather.8.cloned.1.call-done.x_ref, bf16[768,192]{1,0:T(8,128)(2,1)} %bitcast.64, bf16[768,192]{1,0:T(8,128)(2,1)} %bitcast.63, ...), custom_call_target="tpu_custom_call" | custom-call | flops 9663676416 | bytes 8388608 | tf_op jit(solution)/shard_map/attn_fwd/pallas_call | solution.py:146
  103.6 23.2 %swap1.1 = bf16[4,512,192]{2,1,0:T(8,128)(2,1)} custom-call(bf16[4,512,192]{2,1,0:T(8,128)(2,1)} %bitcast.60), custom_call_target="tpu_custom_call" | custom-call | bytes 33554432 | tf_op jit(solution)/shard_map/swap1/pallas_call | solution.py:207
  128.7 16.3 %all-gather.10.cloned.1.call-done = bf16[768,768]{1,0:T(8,128)(2,1)} async-done(((bf16[24,768]{1,0:T(8,128)(2,1)}), bf16[768,768]{1,0:T(8,128)(2,1)}) %all-gather.10.cloned.1.call-update) | async-done | bytes 1179664 | tf_op jit(solution)/shard_map/all_gather | solution.py:266
  148.7 62.4 %all-gather.12.cloned.1.call-done = bf16[3072,768]{1,0:T(8,128)(2,1)} async-done(((bf16[96,768]{1,0:T(8,128)(2,1)}), bf16[3072,768]{1,0:T(8,128)(2,1)}) %all-gather.12.cloned.1.call-update) | async-done | bytes 4718608 | tf_op jit(solution)/shard_map/all_gather | solution.py:266
  211.2 4.4 fusion.27
  221.4 4.2 fusion.18
  225.6 50.8 %all-gather.14.cloned.1.call-done = bf16[3072,768]{1,0:T(8,128)(2,1)} async-done(((bf16[96,768]{1,0:T(8,128)(2,1)}), bf16[3072,768]{1,0:T(8,128)(2,1)}) %all-gather.14.cloned.1.call-update) | async-done | bytes 4718608 | tf_op jit(solution)/shard_map/all_gather | solution.py:266
  276.4 6.3 convert_reduce_fusion
  288.7 6.6 convolution_convert_fusion
  311.5 22.1 %swap2.1 = bf16[4,512,192]{2,1,0:T(8,128)(2,1)} custom-call(bf16[4,512,192]{2,1,0:T(8,128)(2,1)} %bitcast.55), custom_call_target="tpu_custom_call" | custom-call | bytes 33554432 | tf_op jit(solution)/shard_map/swap2/pallas_call | solution.py:207
  333.7 3.2 convolution_convert_fusion.5
  337.2 30.6 %attn_bwd.1 = (bf16[2048,192]{1,0:T(8,128)(2,1)}, bf16[2048,192]{1,0:T(8,128)(2,1)}, bf16[2048,192]{1,0:T(8,128)(2,1)}) custom-call(bf16[2048,192]{1,0:T(8,128)(2,1)} %get-tuple-element.25.q_ref, bf16[2048,192]{1,0:T(8,128)(2,1)} %get-tuple-element.26.k_ref, bf16[2048,192]{1,0:T(8,128)(2,1)} %get-tuple-element.27.v_ref, bf16[2048,192]{1,0:T(8,128)(2,1)} %bitcast.61, ...), custom_call_target="tpu_custom_call" | custom-call | flops 16106127360 | bytes 8388608 | tf_op jit(solution)/shard_map/attn_bwd/pallas_call | solution.py:166
  374.1 20.4 %reduce-scatter.9.cloned.1.call-done = bf16[96,768]{1,0:T(8,128)(2,1)} async-done(((bf16[3072,768]{1,0:T(8,128)(2,1)}), bf16[96,768]{1,0:T(8,128)(2,1)}) %reduce-scatter.9.cloned.1.call-update) | async-done | bytes 147472 | tf_op jit(solution)/shard_map/reduce_scatter | solution.py:313
  394.5 112.3 %reduce-scatter.11.cloned.1.call-done = bf16[96,768]{1,0:T(8,128)(2,1)} async-done(((bf16[3072,768]{1,0:T(8,128)(2,1)}), bf16[96,768]{1,0:T(8,128)(2,1)}) %reduce-scatter.11.cloned.1.call-update) | async-done | bytes 147472 | tf_op jit(solution)/shard_map/reduce_scatter | solution.py:313
  508.4 12.4 %all-reduce.1 = (f32[192]{0:T(256)}, f32[192]{0:T(256)}) all-reduce(f32[192]{0:T(256)S(1)} %convert_reduce_fusion.3, f32[192]{0:T(256)S(1)} %convert_reduce_fusion.2), channel_id=1, replica_groups=mesh['dp'=8,'tensor'=4] {'dp'}, use_global_device_ids=true, to_apply=%region_16.17 | all-reduce | flops 384 | bytes 3072 | tf_op jit(solution)/shard_map/psum | solution.py:336
  520.8 3.2 convolution_bitcast_fusion.1
  528.8 6.8 add_convert_fusion.1
  535.6 72.2 %reduce-scatter.7.cloned.1.call-done = bf16[24,768]{1,0:T(8,128)(2,1)} async-done(((bf16[768,768]{1,0:T(8,128)(2,1)}), bf16[24,768]{1,0:T(8,128)(2,1)}) %reduce-scatter.7.cloned.1.call-update) | async-done | bytes 36880 | tf_op jit(solution)/shard_map/reduce_scatter | solution.py:313
  607.8 9.5 %all_gather.29 = bf16[192,768]{1,0:T(8,128)(2,1)S(1)} all-gather(bf16[24,768]{1,0:T(8,128)(2,1)} %reduce-scatter.7.cloned.1.call-done), channel_id=1, replica_groups=mesh['dp'=8,'tensor'=4] {'dp'}, dimensions={0}, use_global_device_ids=true | all-gather | bytes 331776 | tf_op jit(solution)/shard_map/all_gather | solution.py:316
  618.1 51.3 %reduce-scatter.5.cloned.1.call-done = bf16[512,768]{1,0:T(8,128)(2,1)} async-done(((bf16[2048,768]{1,0:T(8,128)(2,1)}), bf16[512,768]{1,0:T(8,128)(2,1)}) %reduce-scatter.5.cloned.1.call-update) | async-done | bytes 786448 | tf_op jit(solution)/shard_map/reduce_scatter | solution.py:324
  675.3 41.8 %all-reduce = (f32[5,768]{1,0:T(8,128)}, f32[768]{0:T(1024)}, f32[768]{0:T(1024)}, f32[768]{0:T(1024)}, f32[768]{0:T(1024)}, /*index=5*/f32[768]{0:T(1024)}, f32[3072]{0:T(1024)S(1)}, f32[768]{0:T(1024)}) all-reduce(f32[5,768]{1,0:T(8,128)S(1)} %fusion.53, ...), channel_id=1, replica_groups=mesh['dp'=8,'tensor'=4] {'dp','tensor'}, use_global_device_ids=true, to_apply=%region_9.10 | all-reduce | flops 11520 | bytes 92160 | tf_op jit(solution)/shard_map/psum | solution.py:340
  724.6 61.0 %all-reduce.4.cloned.1.call-done = f32[768,3,192]{0,2,1:T(8,128)} async-done(((f32[768,3,192]{0,2,1:T(8,128)}), f32[768,3,192]{0,2,1:T(8,128)}) %all-reduce.4.cloned.1.call-update) | async-done | bytes 1769488 | tf_op jit(solution)/shard_map/psum | solution.py:336
  (145 shorter events, 78.1 us)
Async XLA Ops:
  7.2 7.0 copy-start
  7.2 72.0 %all-gather.8.cloned.1.call-start = ((), (), s32[]{:S(2)}) async-start(), calls=%async_computation.4 | async-start | bytes 3932160 | tf_op jit(solution)/shard_map/all_gather | solution.py:261
  11.5 5.2 copy-start.25
  12.7 132.4 %all-gather.10.cloned.1.call-start = ((), (), s32[]{:S(2)}) async-start(), calls=%async_computation.5 | async-start | bytes 1216512 | tf_op jit(solution)/shard_map/all_gather | solution.py:266
  14.2 197.0 %all-gather.12.cloned.1.call-start = ((), (), s32[]{:S(2)}) async-start(), calls=%async_computation.6 | async-start | bytes 4866048 | tf_op jit(solution)/shard_map/all_gather | solution.py:266
  14.9 261.4 %all-gather.14.cloned.1.call-start = ((), (), s32[]{:S(2)}) async-start(), calls=%async_computation.7 | async-start | bytes 4866048 | tf_op jit(solution)/shard_map/all_gather | solution.py:266
  16.6 377.9 %reduce-scatter.9.cloned.1.call-start = ((), (), s32[]{:S(2)}) async-start(), calls=%async_computation.11 | async-start | bytes 4866048 | tf_op jit(solution)/shard_map/reduce_scatter | solution.py:313
  16.7 4.0 copy-start.21
  103.6 41.5 %copy-start.28 = (f32[768]{0:T(1024)S(1)}, f32[768]{0:T(1024)}, u32[]{:S(2)}) copy-start(f32[768]{0:T(1024)} %param.28) | copy-start | bytes 9220
  148.7 69.7 %copy-start.14 = (bf16[512,768]{1,0:T(8,128)(2,1)}, bf16[512,768]{1,0:T(8,128)(2,1)S(1)}, u32[]{:S(2)}) copy-start(bf16[512,768]{1,0:T(8,128)(2,1)S(1)} %add_convert_fusion.2) | copy-start | bytes 2359300
  211.2 4.4 copy-start.16
  221.4 55.0 %copy-start.13 = (bf16[512,768]{1,0:T(8,128)(2,1)S(1)}, bf16[512,768]{1,0:T(8,128)(2,1)}, u32[]{:S(2)}) copy-start(bf16[512,768]{1,0:T(8,128)(2,1)} %param.35) | copy-start | bytes 2359300
  276.4 6.3 copy-start.15
  288.5 218.3 %reduce-scatter.11.cloned.1.call-start = ((), (), s32[]{:S(2)}) async-start(), calls=%async_computation.13 | async-start | bytes 4866048 | tf_op jit(solution)/shard_map/reduce_scatter | solution.py:313
  295.4 312.4 %reduce-scatter.7.cloned.1.call-start = ((), (), s32[]{:S(2)}) async-start(), calls=%async_computation.10 | async-start | bytes 1216512 | tf_op jit(solution)/shard_map/reduce_scatter | solution.py:313
  336.9 332.6 %reduce-scatter.5.cloned.1.call-start = ((), (), s32[]{:S(2)}) async-start(), calls=%async_computation.8 | async-start | bytes 3932160 | tf_op jit(solution)/shard_map/reduce_scatter | solution.py:324
  337.2 30.6 %copy-start.10 = (bf16[768,3,192]{0,2,1:T(8,128)(2,1)S(1)}, bf16[768,3,192]{0,2,1:T(8,128)(2,1)}, u32[]{:S(2)}) copy-start(bf16[768,3,192]{0,2,1:T(8,128)(2,1)} %param.24) | copy-start | bytes 2654212
  374.0 132.9 %copy-start.5 = (bf16[2048,192]{1,0:T(8,128)(2,1)S(1)}, bf16[2048,192]{1,0:T(8,128)(2,1)}, u32[]{:S(2)}) copy-start(bf16[2048,192]{1,0:T(8,128)(2,1)} %get-tuple-element.29) | copy-start | bytes 2359300
  374.0 343.7 %all-gather.16.cloned.1.call-start = ((), (), s32[]{:S(2)}) async-start(), calls=%async_computation.12 | async-start | bytes 1327104 | tf_op jit(solution)/shard_map/all_gather | solution.py:316
  394.5 327.3 %all-gather.18.cloned.1.call-start = ((), (), s32[]{:S(2)}) async-start(), calls=%async_computation.14 | async-start | bytes 1327104 | tf_op jit(solution)/shard_map/all_gather | solution.py:316
  506.8 278.7 %all-reduce.4.cloned.1.call-start = ((), (), s32[]{:S(2)}) async-start(), calls=%async_computation.9 | async-start | bytes 3538944 | tf_op jit(solution)/shard_map/psum | solution.py:336
  520.8 3.2 copy-start.26
  671.5 3.1 copy-start.22
  785.5 2.9 copy-start.1
  (19 other events, 31.0 us)
Sparse Core Ops, SparseCore 0:
  12.8 66.3 all-gather.7
  82.6 62.3 all-gather.9
  148.5 62.5 all-gather.11
  213.9 62.4 all-gather.13
  288.6 105.7 reduce-scatter.8
  400.7 106.0 reduce-scatter.10
  512.4 95.2 reduce-scatter.6
  610.1 59.3 reduce-scatter.4
  671.4 24.5 all-gather.15
  697.6 24.0 all-gather.17
  725.6 59.8 all-reduce.3
